TPU v7x, 32 devices: a whole 2x2x4 slice. The times are simulated.
32 devices in a mesh: wide: 8 (over z, x), narrow: 4 (over y, core).
Axes of the slice: x: 2, y: 2, z: 4, core: 2. Of those that a mesh axis runs over, the one named last changes fastest.
Arguments:
- table: float32 [256, 256, 64, 128], P(None, 'narrow', 'wide'), may hold values from -200 to 200, as said below
- prior_one: float32 [256, 32], replicated, may hold values from -0.375 to 0.375
- factor_two: float32 [256, 32], replicated, may hold values from -0.375 to 0.375
- factor_three: float32 [64, 32], replicated, may hold values from -0.75 to 0.75
Outputs:
- core: float32 [32, 32, 32, 128], P('narrow', 'wide')
- basis: float32 [256, 32], replicated
Inputs may be any that keep to these rules, and one draw needn't show every extreme that they name: Entries of the table lie within the stated bounds.
All inputs are finite; a program needn't handle non-finite values.
Results may differ from a plain program's by a relative error of at most 0.0003.
Values sent between devices are 32-bit elements; how exact they have to be, the bound alone decides.
A program may use at most 256 MiB of HBM per device.

v0:
```python
import jax
import jax.numpy as jnp
from jax import lax
from jax.sharding import PartitionSpec as P

I2 = 256
I3 = 64
M = 128
SUB = 2


HIGH = lax.Precision.HIGHEST


def orthonormal(q):
    s = jnp.dot(q.T, q, precision=HIGH, preferred_element_type=jnp.float32)
    lower = jnp.linalg.cholesky(s)
    return lax.linalg.triangular_solve(lower, q, left_side=False, lower=True, transpose_a=True)


def per_device(table, prior_one, factor_two, factor_three):
    order_one = table.shape[0]
    rows_two, rows_three, cells = (table.shape[1], table.shape[2], table.shape[3])
    flat = table.reshape(order_one, rows_two * rows_three * cells)
    scale = 1.0 / float(I2 * I3 * M)
    basis = prior_one
    partial_value = jnp.dot(flat, flat.T, precision=HIGH, preferred_element_type=jnp.float32)
    gram = lax.psum(partial_value, ("wide", "narrow")) / scale ** (-1)
    for step in range(SUB):
        basis = orthonormal(
            jnp.dot(gram, basis, precision=HIGH, preferred_element_type=jnp.float32)
        )
    rank = basis.shape[1]
    cut_off = jnp.dot(basis.T, flat, precision=HIGH, preferred_element_type=jnp.float32)
    cut_off = cut_off.reshape(rank, rows_two, rows_three, cells)
    regrouped = lax.all_to_all(cut_off, "narrow", split_axis=0, concat_axis=1, tiled=True)
    second = jnp.einsum("aijm,ib->abjm", regrouped, factor_two, precision=HIGH)
    start = lax.axis_index("wide") * rows_three
    local_three = lax.dynamic_slice_in_dim(factor_three, start, rows_three, 0)
    terms = jnp.einsum("abjm,jc->abcm", second, local_three, precision=HIGH)
    core = lax.psum_scatter(terms, "wide", scatter_dimension=1, tiled=True)
    return (core, basis)


def solution(mesh):
    return jax.shard_map(
        per_device,
        mesh=mesh,
        in_specs=(P(None, "narrow", "wide", None), P(), P(), P()),
        out_specs=(P("narrow", "wide", None, None), P()),
        check_vma=False,
    )
```

profile of v0, /device:TPU:0, one launch (start us, length us, event | category | flops | bytes accessed | tf_op | source)
XLA Modules:
  0.0 652.3 jit_solution(17600477769189699123)
XLA Ops:
  7.2 0.0 copy-start
  7.2 0.0 all-reduce.4.cloned.1.call-start
  7.2 150.5 %fusion.7 = f32[256,256]{1,0:T(8,128)} fusion(f32[256,64,8,128]{3,2,1,0:T(8,128)} %param.7), kind=kOutput, calls=%fused_computation.7 | convolution fusion | flops 51539607552 | bytes 67371008 | tf_op jit(solution)/shard_map/dot_general | solution.py:27
  157.8 0.0 all-reduce.4.cloned.1.call-update
  157.8 56.5 %copy.57 = f32[32,8,512,128]{3,1,2,0:T(8,128)} copy(f32[32,8,512,128]{3,2,1,0:T(8,128)} %bitcast.38) | data formatting | bytes 134217728
  214.2 0.0 copy-start.2
  214.2 65.9 %copy.33 = f32[65536,256]{1,0:T(8,128)} copy(f32[65536,256]{0,1:T(8,128)} %bitcast.74) | data formatting | bytes 134217728 | tf_op jit(solution)/shard_map/dot_general | solution.py:34
  280.2 5.5 all-reduce.4.cloned.1.call-done
  285.6 0.0 copy-done.2
  285.6 1.3 fusion.13
  286.9 0.2 fusion.34
  287.1 0.1 copy.31
  287.2 2.9 cholesky.44
  290.1 0.6 compare_reduce_fusion.1
  290.8 0.7 fusion.20
  291.4 2.4 custom-call.6
  293.9 0.2 convolution_bitcast_fusion.1
  294.1 1.3 fusion.11
  295.4 0.2 fusion.35
  295.6 0.1 copy.32
  295.7 2.9 cholesky.55
  298.6 0.6 compare_reduce_fusion
  299.3 0.7 fusion.21
  299.9 2.4 custom-call.7
  302.4 0.2 fusion.23
  302.6 0.0 copy-start.1
  302.6 63.7 %fusion.18 = f32[32,64,8,128]{3,0,2,1:T(8,128)S(1)} fusion(f32[64,8,128,256]{3,2,1,0:T(8,128)} %bitcast.15, f32[32,256]{1,0:T(8,128)S(1)} %fusion.23), kind=kOutput, calls=%fused_computation.17 | convolution fusion | flops 6442450944 | bytes 75530240 | tf_op jit(solution)/shard_map/dot_general | solution.py:34
  366.4 0.0 copy-done.1
  366.4 8.1 %copy.34 = f32[32,64,8,128]{3,2,1,0:T(8,128)} copy(f32[32,64,8,128]{3,0,2,1:T(8,128)S(1)} %fusion.18) | data formatting | bytes 16777216 | tf_op jit(solution)/shard_map/dot_general | solution.py:34
  374.4 5.7 all-to-all-start
  380.1 0.0 all-reduce.6.cloned.1.call-start
  380.1 93.1 %all-to-all-done = f32[32,64,8,128]{3,2,1,0:T(8,128)} async-done(((f32[32,64,8,128]{3,2,1,0:T(8,128)}), f32[32,64,8,128]{3,2,1,0:T(8,128)}, u32[]{:S(2)}, u32[]{:S(2)}) %all-to-all-start) | async-done | bytes 8388640 | tf_op jit(solution)/shard_map/all_to_all | solution.py:36
  473.3 3.9 copy.35
  477.2 0.0 copy-start.3
  477.2 0.0 copy-done
  477.2 0.0 copy-start.4
  477.3 5.8 fusion.4
  483.0 0.0 copy-done.3
  483.1 5.1 convolution_bitcast_fusion
  488.1 0.0 all-reduce.6.cloned.1.call-update
  488.1 0.0 copy-done.4
  488.1 0.6 dynamic-slice
  489.4 154.2 %all-reduce.6.cloned.1.call-done = f32[8,32,32,128]{3,2,1,0:T(8,128)} async-done(((f32[8,32,32,128]{3,2,1,0:T(8,128)}), f32[8,32,32,128]{3,2,1,0:T(8,128)}) %all-reduce.6.cloned.1.call-update) | async-done | bytes 4194320
  643.6 1.9 constant_dynamic-slice_fusion
  (4 shorter events, 0.1 us)
Async XLA Ops:
  7.2 470.1 %copy-start = (f32[256,32]{0,1:T(8,128)S(1)}, f32[256,32]{0,1:T(8,128)}, u32[]{:S(2)}) copy-start(f32[256,32]{0,1:T(8,128)} %param.9) | copy-start | bytes 98308
  7.2 278.4 %all-reduce.4.cloned.1.call-start = ((), (), s32[]{:S(2)}) async-start(), calls=%async_computation.1 | async-start | bytes 524288 | tf_op jit(solution)/shard_map/psum | solution.py:28
  214.2 71.4 %copy-start.2 = (f32[256,32]{0,1:T(8,128)S(1)}, f32[256,32]{0,1:T(8,128)}, u32[]{:S(2)}) copy-start(f32[256,32]{0,1:T(8,128)} %param.8) | copy-start | bytes 98308
  302.6 63.7 %copy-start.1 = (f32[32,256]{1,0:T(8,128)}, f32[32,256]{1,0:T(8,128)S(1)}, u32[]{:S(2)}) copy-start(f32[32,256]{1,0:T(8,128)S(1)} %fusion.23) | copy-start | bytes 98308
  374.4 98.8 %all-to-all-start = ((f32[32,64,8,128]{3,2,1,0:T(8,128)}), f32[32,64,8,128]{3,2,1,0:T(8,128)}, u32[]{:S(2)}, u32[]{:S(2)}) async-start(f32[32,64,8,128]{3,2,1,0:T(8,128)} %copy.34), calls=%async_computation | async-start | bytes 16777216 | tf_op jit(solution)/shard_map/all_to_all | solution.py:36
  380.1 263.5 %all-reduce.6.cloned.1.call-start = ((), (), s32[]{:S(2)}) async-start(), calls=%async_computation.2 | async-start | bytes 8388608
  477.2 5.8 copy-start.3
  477.2 10.9 %copy-start.4 = (u32[32]{0:T(128)S(1)}, u32[32]{0:T(128)}, u32[]{:S(2)}) copy-start(u32[32]{0:T(128)} %constant.46) | copy-start | bytes 388
Sparse Core Ops, SparseCore 0:
  157.9 127.6 all-reduce.3
  488.3 155.2 all-reduce.5
where the time goes:
time: 653 us; the launch traced here: 652 us
  waiting for transfers between devices  253 us (39%)
  matrix products  228 us (35%)
  local copies, waits for them, and re-layouts  137 us (21%)
  between operations  14.9 us (2%)
  other arithmetic  13.4 us (2%)
    unnamed x3, waiting for transfers between devices  154 us
    dot_general x1, matrix products, per_device(): jnp.dot(flat, flat.T, precision=HIGH, preferred_element_type=jnp.float32)  151 us
    all_to_all x1, waiting for transfers between devices, per_device(): lax.all_to_all(cut_off, 'narrow', split_axis=0, concat_axis=1, tiled=True)  93.1 us
    dot_general x2, local copies, waits for them, and re-layouts, per_device(): jnp.dot(basis.T, flat, precision=HIGH, preferred_element_type=jnp.float32)  74 us
    dot_general x1, matrix products, per_device(): jnp.dot(basis.T, flat, precision=HIGH, preferred_element_type=jnp.float32)  63.7 us
    unnamed x13, local copies, waits for them, and re-layouts  58.9 us
  transfers between devices with their start and end apart: 3, of which 3 were waited for; matrix products, arithmetic and copies ran while one was open for 19% of the time, Pallas kernels for 0%

commit v1 on v0

v1 whole, which is shorter than its diff:
```python
import functools

import jax
import jax.numpy as jnp
from jax import lax
from jax.experimental import pallas as pl
from jax.experimental.pallas import tpu as pltpu
from jax.sharding import PartitionSpec as P

I2 = 256
I3 = 64
M = 128
SUB = 2

F32 = jnp.float32
BF16 = jnp.bfloat16
HIGH = lax.Precision.HIGHEST
NT = (((1,), (1,)), ((), ()))
TN = (((0,), (0,)), ((), ()))


def split(x):
    hi = x.astype(BF16)
    return hi, (x - hi.astype(F32)).astype(BF16)


def gather_rows(ref, first, count, stride, lanes_of):
    flat = ref.reshape(count * stride, ref.shape[-1])
    parts = [flat[pl.ds(first + t, count, stride=stride), :] for t in range(lanes_of)]
    return jnp.concatenate(parts, axis=1)


def gram_kernel(group, table_ref, gram_ref, acc, cross):
    order, rows, _ = table_ref.shape
    step = pl.program_id(0)

    @pl.when(step == 0)
    def _():
        acc[...] = jnp.zeros_like(acc)
        cross[...] = jnp.zeros_like(cross)

    def body(g, carry):
        hi, lo = split(gather_rows(table_ref, g * group, order, rows, group))
        acc[...] += lax.dot_general(hi, hi, NT, preferred_element_type=F32)
        cross[...] += lax.dot_general(hi, lo, NT, preferred_element_type=F32)
        return carry

    lax.fori_loop(0, rows // group, body, 0)

    @pl.when(step == pl.num_programs(0) - 1)
    def _():
        gram_ref[...] = acc[...] + (cross[...] + cross[...].T)


def gram_of(flat):
    order, rows, cells = flat.shape
    block = min(32, rows)
    return pl.pallas_call(
        functools.partial(gram_kernel, min(8, block)),
        grid=(rows // block,),
        in_specs=[pl.BlockSpec((order, block, cells), lambda i: (0, i, 0))],
        out_specs=pl.BlockSpec((order, order), lambda i: (0, 0)),
        out_shape=jax.ShapeDtypeStruct((order, order), F32),
        scratch_shapes=[pltpu.VMEM((order, order), F32)] * 2,
        compiler_params=pltpu.CompilerParams(vmem_limit_bytes=48 << 20),
    )(flat)


def basis_kernel(scale, gram_ref, prior_ref, basis_ref, turned_ref):
    gram = gram_ref[...] * scale
    basis = prior_ref[...]
    rank = basis.shape[1]
    row = lax.broadcasted_iota(jnp.int32, (rank, 1), 0)
    lane = lax.broadcasted_iota(jnp.int32, (rank, rank), 1)
    square_row = lax.broadcasted_iota(jnp.int32, (rank, rank), 0)
    for _ in range(SUB):
        q = jnp.dot(gram, basis, precision=HIGH, preferred_element_type=F32)
        s = lax.dot_general(q, q, TN, precision=HIGH, preferred_element_type=F32)
        inverse = jnp.where(lane == square_row, 1.0, 0.0)
        root = jnp.ones((rank, 1), F32)
        for k in range(rank):
            pivot = s[k : k + 1, k : k + 1]
            root = jnp.where(row == k, lax.rsqrt(pivot), root)
            factor = jnp.where(row > k, s[:, k : k + 1] / pivot, 0.0)
            inverse = inverse - factor * inverse[k : k + 1, :]
            s = s - factor * s[k : k + 1, :]
        inverse = inverse * root
        basis = lax.dot_general(q, inverse, NT, precision=HIGH, preferred_element_type=F32)
    basis_ref[...] = basis
    turned_ref[...] = basis.T


def basis_of(gram, prior):
    scale = 1.0 / float(I2 * I3 * M)
    order, rank = prior.shape
    return pl.pallas_call(
        functools.partial(basis_kernel, scale),
        out_shape=(
            jax.ShapeDtypeStruct((order, rank), F32),
            jax.ShapeDtypeStruct((rank, order), F32),
        ),
    )(gram, prior)


def project_kernel(group, depth, turned_ref, two_ref, table_ref, out_ref, trunc):
    order, rows, cells = table_ref.shape
    rank = turned_ref.shape[0]
    total = trunc.shape[0] // rank
    tall = total // depth
    step = pl.program_id(0)
    left_hi, left_lo = split(turned_ref[...])
    left = jnp.concatenate([left_hi, left_lo], axis=0)

    def body(g, carry):
        hi, lo = split(gather_rows(table_ref, g * group, order, rows, group))
        both = jnp.dot(left, hi, preferred_element_type=F32)
        value = both[:rank] + (both[rank:] + jnp.dot(left_hi, lo, preferred_element_type=F32))
        for t in range(group):
            place = step * rows + g * group + t
            place = lax.rem(place, depth) * tall + place // depth
            trunc[pl.ds(place, rank, stride=total), :] = value[:, t * cells : (t + 1) * cells]
        return carry

    lax.fori_loop(0, rows // group, body, 0)

    @pl.when(step == pl.num_programs(0) - 1)
    def _():
        two_hi, two_lo = split(two_ref[...])
        two = jnp.concatenate([two_hi, two_lo], axis=0)
        width = two_ref.shape[0]

        def second(r, carry):
            parts = [
                trunc[pl.ds(pl.multiple_of(r * total + j * tall, tall), tall), :]
                for j in range(depth)
            ]
            hi, lo = split(jnp.concatenate(parts, axis=1))
            both = jnp.dot(two, hi, preferred_element_type=F32)
            value = both[:width] + (both[width:] + jnp.dot(two_hi, lo, preferred_element_type=F32))
            for j in range(depth):
                out_ref[pl.ds(r * width * depth + j, width, stride=depth), :] = value[
                    :, j * cells : (j + 1) * cells
                ]
            return carry

        lax.fori_loop(0, rank, second, 0)


def project(turned, two, flat, depth):
    order, rows, cells = flat.shape
    rank, width = turned.shape[0], two.shape[0]
    block = min(32, rows)
    return pl.pallas_call(
        functools.partial(project_kernel, min(8, block), depth),
        grid=(rows // block,),
        in_specs=[
            pl.BlockSpec(turned.shape, lambda i: (0, 0)),
            pl.BlockSpec(two.shape, lambda i: (0, 0)),
            pl.BlockSpec((order, block, cells), lambda i: (0, i, 0)),
        ],
        out_specs=pl.BlockSpec((rank * width * depth, cells), lambda i: (0, 0)),
        out_shape=jax.ShapeDtypeStruct((rank * width * depth, cells), F32),
        scratch_shapes=[pltpu.VMEM((rank * rows, cells), F32)],
        compiler_params=pltpu.CompilerParams(vmem_limit_bytes=56 << 20),
    )(turned, two, flat)


def per_device(narrow, wide, table, prior_one, factor_two, factor_three):
    order, rows_two, rows_three, cells = table.shape
    rank = prior_one.shape[1]
    width = factor_two.shape[1]
    flat = table.reshape(order, rows_two * rows_three, cells)
    gram = lax.psum(gram_of(flat), ("wide", "narrow"))
    basis, turned = basis_of(gram, prior_one)
    at = lax.axis_index("narrow")
    two = lax.dynamic_slice_in_dim(factor_two, at * rows_two, rows_two, 0).T
    part = project(turned, two, flat, rows_three)
    chips = narrow // 2
    core = at % 2
    part = part.reshape(chips, 2, rank // narrow, width, rows_three, cells)
    keep = lax.dynamic_index_in_dim(part, core, 1, keepdims=False)
    give = lax.dynamic_index_in_dim(part, 1 - core, 1, keepdims=False)
    swap = [(i, i ^ 1) for i in range(narrow)]
    part = keep + lax.ppermute(give, "narrow", swap)
    chip = at // 2
    mine = lax.dynamic_index_in_dim(part, chip, 0, keepdims=False)
    for hop in range(1, chips):
        perm = [(i, (i + 2 * hop) % narrow) for i in range(narrow)]
        there = lax.dynamic_index_in_dim(part, (chip + hop) % chips, 0, keepdims=False)
        mine = mine + lax.ppermute(there, "narrow", perm)
    mine = mine.reshape(rank // narrow, wide, width // wide, rows_three, cells)
    spread = lax.all_to_all(mine, "wide", split_axis=1, concat_axis=1, tiled=True)
    three = factor_three.reshape(wide, rows_three, factor_three.shape[1])
    core_out = jnp.einsum("rwbjm,wjc->rbcm", spread, three, precision=HIGH)
    return core_out, basis


def solution(mesh):
    return jax.shard_map(
        functools.partial(per_device, mesh.shape["narrow"], mesh.shape["wide"]),
        mesh=mesh,
        in_specs=(P(None, "narrow", "wide", None), P(), P(), P()),
        out_specs=(P("narrow", "wide", None, None), P()),
        check_vma=False,
    )
```

time: 653 us -> 347 us (0.53)
  matrix products: 228 us -> 0.7 us
  Pallas kernels: 0 us -> 137 us
  local copies, waits for them, and re-layouts: 137 us -> 5.91 us
  waiting for transfers between devices: 253 us -> 179 us
  other arithmetic: 13.4 us -> 3.78 us
    dot_general x8 -> x1, matrix products: 228 us -> 0.7 us  [per_device(): core_out = jnp.einsum('rwbjm,wjc->rbcm', spread, three, precision=HIGH)]
    unnamed x3 -> x1, waiting for transfers between devices: 154 us -> 0.02 us
    pallas_call x0 -> x3, Pallas kernels: none -> 137 us  [the longest x1 71 us: project(): pl.pallas_call(functools.partial(project_kernel, min(8, block), depth), g...]
    psum x1, waiting for transfers between devices: 5.47 us -> 126 us  [per_device(): gram = lax.psum(gram_of(flat), ('wide', 'narrow'))]
    dot_general x4 -> x1, local copies, waits for them, and re-layouts: 74.1 us -> 0.84 us  [per_device(): core_out = jnp.einsum('rwbjm,wjc->rbcm', spread, three, precision=HIGH)]
    all_to_all x1, waiting for transfers between devices: 93.1 us -> 24.7 us  [per_device(): lax.all_to_all(mine, 'wide', split_axis=1, concat_axis=1, tiled=True)]
    unnamed x13 -> x11, local copies, waits for them, and re-layouts: 58.9 us -> 1.54 us
    ppermute x0 -> x2, waiting for transfers between devices: none -> 28.1 us  [the longest x1 23.8 us: per_device(): mine = mine + lax.ppermute(there, 'narrow', perm)]
  transfers between devices with their start and end apart: 3 -> 4, of which waited for: 3 -> 4; matrix products, arithmetic and copies ran while one was open for 19% -> 1% of each run, Pallas kernels for 0% -> 0%
where the time goes in v1:
time: 347 us
  waiting for transfers between devices  179 us (52%)
  Pallas kernels  137 us (39%)
  between operations  14.2 us (4%)
  starting transfers between devices  6.1 us (2%)
  local copies, waits for them, and re-layouts  5.91 us (2%)
  other arithmetic  3.78 us (1%)
    psum x1, waiting for transfers between devices, per_device(): gram = lax.psum(gram_of(flat), ('wide', 'narrow'))  126 us
    pallas_call x1, Pallas kernels, project(): pl.pallas_call(functools.partial(project_kernel, min(8, block), depth), g...  71 us
    pallas_call x1, Pallas kernels, gram_of(): pl.pallas_call(functools.partial(gram_kernel, min(8, block)), grid=(rows...  56.7 us
    all_to_all x1, waiting for transfers between devices, per_device(): lax.all_to_all(mine, 'wide', split_axis=1, concat_axis=1, tiled=True)  24.7 us
    ppermute x1, waiting for transfers between devices, per_device(): mine = mine + lax.ppermute(there, 'narrow', perm)  23.8 us
    pallas_call x1, Pallas kernels, basis_of(): pl.pallas_call(functools.partial(basis_kernel, scale), out_shape=(jax.Sha...  9.37 us
  transfers between devices with their start and end apart: 4, of which 4 were waited for; matrix products, arithmetic and copies ran while one was open for 1% of the time, Pallas kernels for 0%

profile of v1, /device:TPU:0, one launch (start us, length us, event | category | flops | bytes accessed | tf_op | source)
XLA Modules:
  0.0 346.8 jit_solution(11846265487567949852)
XLA Ops:
  7.2 0.0 copy-start
  7.2 0.0 all-reduce.2.cloned.1.call-start
  7.2 0.0 copy-start.2
  7.2 56.7 %shard_map.59 = f32[256,256]{1,0:T(8,128)} custom-call(f32[256,512,128]{2,1,0:T(8,128)} %bitcast.table_ref), custom_call_target="tpu_custom_call" | custom-call | tf_op jit(solution)/shard_map/pallas_call | solution.py:58
  63.9 0.0 all-reduce.2.cloned.1.call-update
  63.9 0.0 copy-done.2
  64.0 0.7 copy.14.prior_ref
  64.7 0.0 copy-done
  64.7 0.7 dynamic-slice_bitcast_fusion.2.two_ref
  65.4 126.4 %all-reduce.2.cloned.1.call-done.gram_ref = f32[256,256]{1,0:T(8,128)} async-done(((f32[256,256]{1,0:T(8,128)}), f32[256,256]{1,0:T(8,128)}) %all-reduce.2.cloned.1.call-update) | async-done | bytes 262160 | tf_op jit(solution)/shard_map/psum | solution.py:173
  191.7 9.4 %shard_map.60 = (f32[256,32]{1,0:T(8,128)}, f32[32,256]{1,0:T(8,128)}) custom-call(f32[256,256]{1,0:T(8,128)} %all-reduce.2.cloned.1.call-done.gram_ref, f32[256,32]{1,0:T(8,128)} %copy.14.prior_ref), custom_call_target="tpu_custom_call" | custom-call | tf_op jit(solution)/shard_map/pallas_call | solution.py:96
  201.1 71.0 %shard_map.61 = f32[8192,128]{1,0:T(8,128)} custom-call(f32[32,256]{1,0:T(8,128)} %get-tuple-element.4.turned_ref, f32[32,64]{1,0:T(8,128)} %dynamic-slice_bitcast_fusion.2.two_ref, f32[256,512,128]{2,1,0:T(8,128)} %bitcast.table_ref), custom_call_target="tpu_custom_call" | custom-call | tf_op jit(solution)/shard_map/pallas_call | solution.py:153
  272.1 1.7 dynamic-slice_bitcast_fusion
  273.8 0.1 collective-permute-start
  273.9 4.2 %collective-permute-done = f32[2,8,32,8,128]{4,3,2,1,0:T(8,128)} collective-permute-done((f32[2,8,32,8,128]{4,3,2,1,0:T(8,128)S(1)}, f32[2,8,32,8,128]{4,3,2,1,0:T(8,128)}, u32[]{:S(2)}, u32[]{:S(2)}) %collective-permute-start) | collective-permute-done | bytes 2097184 | tf_op jit(solution)/shard_map/ppermute | solution.py:184
  278.2 2.4 bitcast_add_fusion
  280.6 0.1 dynamic-slice_bitcast_fusion.1
  280.7 1.5 collective-permute-start.1
  282.2 23.8 %collective-permute-done.1 = f32[8,32,8,128]{3,2,1,0:T(8,128)} collective-permute-done((f32[8,32,8,128]{3,2,1,0:T(8,128)S(1)}, f32[8,32,8,128]{3,2,1,0:T(8,128)}, u32[]{:S(2)}, u32[]{:S(2)}) %collective-permute-start.1) | collective-permute-done | bytes 1048608 | tf_op jit(solution)/shard_map/ppermute | solution.py:190
  306.1 1.3 bitcast_add_fusion.1
  307.4 0.0 copy-start.3
  307.4 0.0 copy-start.1
  307.4 1.1 copy.15
  308.5 4.5 %all-to-all-start = ((f32[8,8,4,8,128]{4,3,2,0,1:T(8,128)}), f32[8,8,4,8,128]{4,3,2,0,1:T(8,128)S(1)}, u32[]{:S(2)}, u32[]{:S(2)}) async-start(f32[8,8,4,8,128]{4,3,2,0,1:T(8,128)} %copy.15), calls=%async_computation | async-start | bytes 2097152 | tf_op jit(solution)/shard_map/all_to_all | solution.py:192
  313.0 0.0 copy-done.3
  313.0 0.1 copy.16
  313.1 0.0 copy-done.1
  313.1 0.7 copy.19
  313.7 24.7 %all-to-all-done = f32[8,8,4,8,128]{4,3,2,0,1:T(8,128)S(1)} async-done(((f32[8,8,4,8,128]{4,3,2,0,1:T(8,128)}), f32[8,8,4,8,128]{4,3,2,0,1:T(8,128)S(1)}, u32[]{:S(2)}, u32[]{:S(2)}) %all-to-all-start) | async-done | bytes 1048608 | tf_op jit(solution)/shard_map/all_to_all | solution.py:192
  338.4 0.7 fusion
  339.1 0.8 copy.29
Async XLA Ops:
  7.2 57.5 %copy-start = (f32[256,32]{0,1:T(8,128)S(1)}, f32[256,32]{0,1:T(8,128)}, u32[]{:S(2)}) copy-start(f32[256,32]{0,1:T(8,128)} %param.6) | copy-start | bytes 98308
  7.2 184.6 %all-reduce.2.cloned.1.call-start = ((), (), s32[]{:S(2)}) async-start(), calls=%async_computation.1 | async-start | bytes 524288 | tf_op jit(solution)/shard_map/psum | solution.py:173
  7.2 56.7 %copy-start.2 = (f32[256,32]{0,1:T(8,128)S(1)}, f32[256,32]{0,1:T(8,128)}, u32[]{:S(2)}) copy-start(f32[256,32]{0,1:T(8,128)} %param.5) | copy-start | bytes 98308
  273.8 4.4 %collective-permute-start = (f32[2,8,32,8,128]{4,3,2,1,0:T(8,128)S(1)}, f32[2,8,32,8,128]{4,3,2,1,0:T(8,128)}, u32[]{:S(2)}, u32[]{:S(2)}) collective-permute-start(f32[2,8,32,8,128]{4,3,2,1,0:T(8,128)S(1)} %dynamic-slice_bitcast_fusion), channel_id=1, source_target_pairs={{0,1},{1,0},{2,3},{3,2},{4,5},{5,4},{6,7},{7,6},{8,9},{9,8},{10,11... | collective-permute-start | bytes 6291464 | tf_op jit(solution)/shard_map/ppermute | solution.py:184
  280.7 25.4 %collective-permute-start.1 = (f32[8,32,8,128]{3,2,1,0:T(8,128)S(1)}, f32[8,32,8,128]{3,2,1,0:T(8,128)}, u32[]{:S(2)}, u32[]{:S(2)}) collective-permute-start(f32[8,32,8,128]{3,2,1,0:T(8,128)S(1)} %dynamic-slice_bitcast_fusion.1), channel_id=1, source_target_pairs={{0,2},{1,3},{2,0},{3,1},{4,6},{5,7},{6,4},{7,5},{8,10},{9,11},{10,... | collective-permute-start | bytes 3145736 | tf_op jit(solution)/shard_map/ppermute | solution.py:190
  307.4 5.5 %copy-start.3 = (f32[64,32]{0,1:T(8,128)S(1)}, f32[64,32]{0,1:T(8,128)}, u32[]{:S(2)}) copy-start(f32[64,32]{0,1:T(8,128)} %param.7) | copy-start | bytes 24580
  307.4 5.6 %copy-start.1 = (f32[256,32]{1,0:T(8,128)S(1)}, f32[256,32]{1,0:T(8,128)}, u32[]{:S(2)}) copy-start(f32[256,32]{1,0:T(8,128)} %get-tuple-element.11) | copy-start | bytes 98308
  308.5 29.9 %all-to-all-start = ((f32[8,8,4,8,128]{4,3,2,0,1:T(8,128)}), f32[8,8,4,8,128]{4,3,2,0,1:T(8,128)S(1)}, u32[]{:S(2)}, u32[]{:S(2)}) async-start(f32[8,8,4,8,128]{4,3,2,0,1:T(8,128)} %copy.15), calls=%async_computation | async-start | bytes 2097152 | tf_op jit(solution)/shard_map/all_to_all | solution.py:192
Sparse Core Ops, SparseCore 0:
  64.0 127.6 all-reduce.1

commit v2 on v1

v2 whole, which is shorter than its diff:
```python
import functools

import jax
import jax.numpy as jnp
from jax import lax
from jax.experimental import pallas as pl
from jax.experimental.pallas import tpu as pltpu
from jax.sharding import PartitionSpec as P

I2 = 256
I3 = 64
M = 128
SUB = 2

F32 = jnp.float32
BF16 = jnp.bfloat16
HIGH = lax.Precision.HIGHEST
NT = (((1,), (1,)), ((), ()))
TN = (((0,), (0,)), ((), ()))
MESH = pl.DeviceIdType.MESH


def split(x):
    hi = x.astype(BF16)
    return hi, (x - hi.astype(F32)).astype(BF16)


def gather_rows(ref, first, group):
    block = jnp.swapaxes(ref[:, pl.ds(pl.multiple_of(first, group), group), :], 0, 1)
    return jnp.concatenate([block[t] for t in range(group)], axis=1)


def gram_kernel(group, table_ref, gram_ref, acc, cross):
    rows = table_ref.shape[1]
    step = pl.program_id(0)

    @pl.when(step == 0)
    def _():
        acc[...] = jnp.zeros_like(acc)
        cross[...] = jnp.zeros_like(cross)

    def body(g, carry):
        hi, lo = split(gather_rows(table_ref, g * group, group))
        acc[...] += lax.dot_general(hi, hi, NT, preferred_element_type=F32)
        cross[...] += lax.dot_general(hi, lo, NT, preferred_element_type=F32)
        return carry

    lax.fori_loop(0, rows // group, body, 0)

    @pl.when(step == pl.num_programs(0) - 1)
    def _():
        gram_ref[...] = acc[...] + (cross[...] + cross[...].T)


def gram_of(flat):
    order, rows, cells = flat.shape
    block = min(32, rows)
    return pl.pallas_call(
        functools.partial(gram_kernel, min(16, block)),
        grid=(rows // block,),
        in_specs=[pl.BlockSpec((order, block, cells), lambda i: (0, i, 0))],
        out_specs=pl.BlockSpec((order, order), lambda i: (0, 0)),
        out_shape=jax.ShapeDtypeStruct((order, order), F32),
        scratch_shapes=[pltpu.VMEM((order, order), F32)] * 2,
        compiler_params=pltpu.CompilerParams(vmem_limit_bytes=48 << 20),
    )(flat)


def greet(narrow, wide, at, place):
    barrier = pltpu.get_barrier_semaphore()
    for d in range(1, narrow):
        pl.semaphore_signal(
            barrier, inc=1, device_id={"narrow": lax.rem(at + d, narrow)}, device_id_type=MESH
        )
    for d in range(1, wide):
        pl.semaphore_signal(
            barrier, inc=1, device_id={"wide": lax.rem(place + d, wide)}, device_id_type=MESH
        )


def send(src, dst, send_sem, recv_sem, axis, to):
    copy = pltpu.make_async_remote_copy(
        src_ref=src,
        dst_ref=dst,
        send_sem=send_sem,
        recv_sem=recv_sem,
        device_id={axis: to},
        device_id_type=MESH,
    )
    copy.start()
    return copy


def finish(copies):
    for copy in copies:
        copy.wait()


def basis_kernel(
    narrow, wide, scale, part_ref, prior_ref, basis_ref, turned_ref,
    box_n, mine, box_w, full, square, sn, rn, sw, rw, tw, vw, tn, vn,
):
    at, place = lax.axis_index("narrow"), lax.axis_index("wide")
    greet(narrow, wide, at, place)
    pl.semaphore_wait(pltpu.get_barrier_semaphore(), narrow + wide - 2)
    copies = []
    for d in range(1, narrow):
        to = lax.rem(at + d, narrow)
        copies.append(send(part_ref.at[to], box_n.at[d], sn.at[d], rn.at[d], "narrow", to))
    finish(copies)
    value = part_ref[at]
    for d in range(1, narrow):
        value = value + box_n[d]
    mine[...] = value
    copies = []
    for d in range(1, wide):
        to = lax.rem(place + d, wide)
        copies.append(send(mine.at[to], box_w.at[d], sw.at[d], rw.at[d], "wide", to))
    finish(copies)
    value = mine[place]
    for d in range(1, wide):
        value = value + box_w[d]
    full[at, place] = value * scale
    copies = []
    for d in range(1, wide):
        to = lax.rem(place + d, wide)
        own = full.at[at, place]
        copies.append(send(own, own, tw.at[d], vw.at[d], "wide", to))
    finish(copies)
    copies = []
    for d in range(1, narrow):
        to = lax.rem(at + d, narrow)
        own = full.at[at]
        copies.append(send(own, own, tn.at[d], vn.at[d], "narrow", to))
    finish(copies)
    small = full.shape[2]
    for i in range(narrow * wide):
        square[i * small : (i + 1) * small, :] = full[i // wide, i % wide]
    gram = square[...]
    basis = prior_ref[...]
    rank = basis.shape[1]
    row = lax.broadcasted_iota(jnp.int32, (rank, 1), 0)
    lane = lax.broadcasted_iota(jnp.int32, (rank, rank), 1)
    square_row = lax.broadcasted_iota(jnp.int32, (rank, rank), 0)
    for _ in range(SUB):
        q = jnp.dot(gram, basis, precision=HIGH, preferred_element_type=F32)
        s = lax.dot_general(q, q, TN, precision=HIGH, preferred_element_type=F32)
        inverse = jnp.where(lane == square_row, 1.0, 0.0)
        root = jnp.ones((rank, 1), F32)
        for k in range(rank):
            pivot = s[k : k + 1, k : k + 1]
            root = jnp.where(row == k, lax.rsqrt(pivot), root)
            factor = jnp.where(row > k, s[:, k : k + 1] / pivot, 0.0)
            inverse = inverse - factor * inverse[k : k + 1, :]
            s = s - factor * s[k : k + 1, :]
        inverse = inverse * root
        basis = lax.dot_general(q, inverse, NT, precision=HIGH, preferred_element_type=F32)
    basis_ref[...] = basis
    turned_ref[...] = basis.T


def basis_of(narrow, wide, gram, prior):
    scale = 1.0 / float(I2 * I3 * M)
    order, rank = prior.shape
    small = order // (narrow * wide)
    dma = pltpu.SemaphoreType.DMA
    return pl.pallas_call(
        functools.partial(basis_kernel, narrow, wide, scale),
        in_specs=[pl.BlockSpec(memory_space=pltpu.VMEM)] * 2,
        out_specs=[pl.BlockSpec(memory_space=pltpu.VMEM)] * 2,
        out_shape=(
            jax.ShapeDtypeStruct((order, rank), F32),
            jax.ShapeDtypeStruct((rank, order), F32),
        ),
        scratch_shapes=[
            pltpu.VMEM((narrow, wide, small, order), F32),
            pltpu.VMEM((wide, small, order), F32),
            pltpu.VMEM((wide, small, order), F32),
            pltpu.VMEM((narrow, wide, small, order), F32),
            pltpu.VMEM((order, order), F32),
            dma((narrow,)), dma((narrow,)),
            dma((wide,)), dma((wide,)),
            dma((wide,)), dma((wide,)),
            dma((narrow,)), dma((narrow,)),
        ],
        compiler_params=pltpu.CompilerParams(collective_id=1, has_side_effects=True),
    )(gram.reshape(narrow, wide, small, order), prior)


def project_kernel(
    group, depth, narrow, wide, spread, turned_ref, two_ref, table_ref, out_ref,
    trunc, second, core_box, chip_box, wide_box, sc, rc, sy, ry, sw, rw,
):
    _, rows, cells = table_ref.shape
    rank = turned_ref.shape[0]
    total = trunc.shape[0] // rank
    tall = total // depth
    step = pl.program_id(0)
    at, place = lax.axis_index("narrow"), lax.axis_index("wide")

    @pl.when(step == 0)
    def _():
        greet(narrow, wide, at, place)

    left_hi, left_lo = split(turned_ref[...])
    left = jnp.concatenate([left_hi, left_lo], axis=0)

    def body(g, carry):
        hi, lo = split(gather_rows(table_ref, g * group, group))
        both = jnp.dot(left, hi, preferred_element_type=F32)
        value = both[:rank] + (both[rank:] + jnp.dot(left_hi, lo, preferred_element_type=F32))
        for t in range(group):
            spot = step * rows + g * group + t
            spot = lax.rem(spot, depth) * tall + spot // depth
            trunc[pl.ds(spot, rank, stride=total), :] = value[:, t * cells : (t + 1) * cells]
        return carry

    lax.fori_loop(0, rows // group, body, 0)

    @pl.when(step == pl.num_programs(0) - 1)
    def _():
        pl.semaphore_wait(pltpu.get_barrier_semaphore(), narrow + wide - 2)
        two_hi, two_lo = split(two_ref[...])
        two = jnp.concatenate([two_hi, two_lo], axis=0)
        width = two_ref.shape[0]
        per = rank // narrow
        slab = width * depth
        chips = narrow // 2
        chip, core = at // 2, lax.rem(at, 2)
        chunk = 2 if per % 2 == 0 else 1
        chunks = per // chunk
        flat = second.reshape(rank * slab, cells)

        def compute(block, q):
            def one(k, carry):
                r = block * per + q * chunk + k
                parts = [
                    trunc[pl.ds(pl.multiple_of(r * total + j * tall, tall), tall), :]
                    for j in range(depth)
                ]
                hi, lo = split(jnp.concatenate(parts, axis=1))
                both = jnp.dot(two, hi, preferred_element_type=F32)
                value = both[:width] + (
                    both[width:] + jnp.dot(two_hi, lo, preferred_element_type=F32)
                )
                for j in range(depth):
                    flat[pl.ds(r * slab + j, width, stride=depth), :] = value[
                        :, j * cells : (j + 1) * cells
                    ]
                return carry

            lax.fori_loop(0, chunk, one, 0)

        def part(q):
            return pl.ds(q * chunk, chunk)

        def target(h):
            return lax.rem(chip + h, chips)

        to_core, to_chip, to_wide = {}, {}, []

        def start(h, q):
            other = target(h) * 2 + (1 - core)
            compute(other, q)
            to_core[h, q] = send(
                second.at[other, part(q)], core_box.at[h, part(q)],
                sc.at[h, q], rc.at[h, q], "narrow", chip * 2 + (1 - core),
            )
            compute(target(h) * 2 + core, q)

        def merge(h, q):
            to_core[h, q].wait_recv()
            block = target(h) * 2 + core
            second[block, part(q)] = second[block, part(q)] + core_box[h, part(q)]
            if h:
                to_chip[h, q] = send(
                    second.at[block, part(q)], chip_box.at[h - 1, part(q)],
                    sy.at[h, q], ry.at[h, q], "narrow", block,
                )

        pairs = [(h, q) for h in [*range(1, chips), 0] for q in range(chunks)]
        for i, pair in enumerate(pairs):
            start(*pair)
            if i:
                merge(*pairs[i - 1])
        merge(*pairs[-1])
        for q in range(chunks):
            value = second[at, part(q)]
            for h in range(1, chips):
                to_chip[h, q].wait_recv()
                value = value + chip_box[h - 1, part(q)]
            if not spread:
                out_ref[0, part(q)] = value
                continue
            second[at, part(q)] = value
            band = slab // wide
            for d in range(1, wide):
                to = lax.rem(place + d, wide)
                rows_to = pl.ds(pl.multiple_of(to * band, band), band)
                to_wide.append(
                    send(
                        second.at[at, part(q), rows_to], wide_box.at[place, part(q)],
                        sw.at[d, q], rw.at[d, q], "wide", to,
                    )
                )
            own = pl.ds(pl.multiple_of(place * band, band), band)
            out_ref[place, part(q)] = second[at, part(q), own]
        for copy in [*to_core.values(), *to_chip.values()]:
            copy.wait_send()
        finish(to_wide)
        if spread:
            for d in range(1, wide):
                source = lax.rem(place + d, wide)
                out_ref[source] = wide_box[source]


def project(narrow, wide, turned, two, flat, depth):
    order, rows, cells = flat.shape
    rank, width = turned.shape[0], two.shape[0]
    block = min(32, rows)
    per, slab, chips = rank // narrow, width * depth, narrow // 2
    spread = (slab // wide) % 8 == 0
    shape = (wide, per, slab // wide, cells) if spread else (1, per, slab, cells)
    chunks = per // 2 if per % 2 == 0 else per
    dma = pltpu.SemaphoreType.DMA
    out = pl.pallas_call(
        functools.partial(
            project_kernel, min(16, block), depth, narrow, wide, spread
        ),
        grid=(rows // block,),
        in_specs=[
            pl.BlockSpec(turned.shape, lambda i: (0, 0)),
            pl.BlockSpec(two.shape, lambda i: (0, 0)),
            pl.BlockSpec((order, block, cells), lambda i: (0, i, 0)),
        ],
        out_specs=pl.BlockSpec(shape, lambda i: (0, 0, 0, 0)),
        out_shape=jax.ShapeDtypeStruct(shape, F32),
        scratch_shapes=[
            pltpu.VMEM((rank * rows, cells), F32),
            pltpu.VMEM((narrow, per, slab, cells), F32),
            pltpu.VMEM((chips, per, slab, cells), F32),
            pltpu.VMEM((max(chips - 1, 1), per, slab, cells), F32),
            pltpu.VMEM(shape, F32),
            dma((chips, chunks)), dma((chips, chunks)),
            dma((chips, chunks)), dma((chips, chunks)),
            dma((wide, chunks)), dma((wide, chunks)),
        ],
        compiler_params=pltpu.CompilerParams(
            vmem_limit_bytes=56 << 20, collective_id=2, has_side_effects=True
        ),
    )(turned, two, flat)
    if not spread:
        out = out.reshape(per, wide, slab // wide, cells)
        out = lax.all_to_all(out, "wide", split_axis=1, concat_axis=1, tiled=True)
        out = out.transpose(1, 0, 2, 3)
    return out.reshape(wide, per, width // wide, depth, cells)


def per_device(narrow, wide, table, prior_one, factor_two, factor_three):
    order, rows_two, rows_three, cells = table.shape
    flat = table.reshape(order, rows_two * rows_three, cells)
    basis, turned = basis_of(narrow, wide, gram_of(flat), prior_one)
    at = lax.axis_index("narrow")
    two = lax.dynamic_slice_in_dim(factor_two, at * rows_two, rows_two, 0).T
    spread = project(narrow, wide, turned, two, flat, rows_three)
    three = factor_three.reshape(wide, rows_three, factor_three.shape[1])
    core_out = jnp.einsum("wrbjm,wjc->rbcm", spread, three, precision=HIGH)
    return core_out, basis


def solution(mesh):
    return jax.shard_map(
        functools.partial(per_device, mesh.shape["narrow"], mesh.shape["wide"]),
        mesh=mesh,
        in_specs=(P(None, "narrow", "wide", None), P(), P(), P()),
        out_specs=(P("narrow", "wide", None, None), P()),
        check_vma=False,
    )
```

time: 347 us -> 152 us (0.44)
  waiting for transfers between devices: 179 us -> 0 us
  between operations: 14.2 us -> 0.68 us
  starting transfers between devices: 6.1 us -> 0 us
  Pallas kernels: 137 us -> 141 us
  other arithmetic: 3.78 us -> 0 us
    psum x1 -> x0, waiting for transfers between devices: 126 us -> none  [per_device(): gram = lax.psum(gram_of(flat), ('wide', 'narrow'))]
    ppermute x2 -> x0, waiting for transfers between devices: 28.1 us -> none  [the longest x1 23.8 us: per_device(): mine = mine + lax.ppermute(there, 'narrow', perm)]
    all_to_all x1 -> x0, waiting for transfers between devices: 24.7 us -> none  [per_device(): lax.all_to_all(mine, 'wide', split_axis=1, concat_axis=1, tiled=True)]
    all_to_all x1 -> x0, starting transfers between devices: 4.46 us -> none  [per_device(): lax.all_to_all(mine, 'wide', split_axis=1, concat_axis=1, tiled=True)]
    pallas_call x3, Pallas kernels: 137 us -> 141 us  [the longest x1 71.6 us: project(): pl.pallas_call(functools.partial(project_kernel, min(16, block), depth, n...]
    unnamed x11 -> x7, local copies, waits for them, and re-layouts: 1.54 us -> 5.35 us
    add x2 -> x0, other arithmetic: 3.78 us -> none  [the longest x1 2.44 us: per_device(): part = keep + lax.ppermute(give, 'narrow', swap)]
  transfers between devices with their start and end apart: 4 -> 0, of which waited for: 4 -> 0; matrix products, arithmetic and copies ran while one was open for 1% -> 0% of each run, Pallas kernels for 0% -> 0%
where the time goes in v2:
time: 152 us; the launch traced here: 150 us
  Pallas kernels  141 us (93%)
  local copies, waits for them, and re-layouts  6.85 us (5%)
  matrix products  1.91 us (1%)
    pallas_call x1, Pallas kernels, project(): pl.pallas_call(functools.partial(project_kernel, min(16, block), depth, n...  71.6 us
    pallas_call x1, Pallas kernels, gram_of(): pl.pallas_call(functools.partial(gram_kernel, min(16, block)), grid=(rows...  37.9 us
    pallas_call x1, Pallas kernels, basis_of(): pl.pallas_call(functools.partial(basis_kernel, narrow, wide, scale), in_s...  31.4 us
    unnamed x7, local copies, waits for them, and re-layouts  5.35 us

profile of v2, /device:TPU:0, one launch (start us, length us, event | category | flops | bytes accessed | tf_op | source)
XLA Modules:
  0.0 150.4 jit_solution(13930716880284747621)
XLA Ops:
  0.6 0.0 copy-start
  0.6 0.7 copy-done
  1.4 0.7 dynamic-slice_bitcast_fusion.two_ref
  2.1 0.8 copy.11
  2.9 1.5 %copy.10.prior_ref = f32[256,32]{1,0:T(8,128)} copy(f32[256,32]{0,1:T(8,128)} %param.5) | data formatting | bytes 65536 | tf_op args[1]
  4.4 37.9 %shard_map.59 = f32[256,256]{1,0:T(8,128)S(1)} custom-call(f32[256,512,128]{2,1,0:T(8,128)} %bitcast.table_ref), custom_call_target="tpu_custom_call" | custom-call | tf_op jit(solution)/shard_map/pallas_call | solution.py:58
  42.3 0.0 copy-start.1
  42.3 0.7 copy-done.1
  43.0 31.4 %shard_map.60 = (f32[256,32]{1,0:T(8,128)}, f32[32,256]{1,0:T(8,128)}) custom-call(f32[4,8,8,256]{3,2,1,0:T(8,128)} %bitcast.20, f32[256,32]{1,0:T(8,128)} %copy.10.prior_ref), custom_call_target="tpu_custom_call" | custom-call | tf_op jit(solution)/shard_map/pallas_call | solution.py:167
  74.4 1.6 %copy.14 = f32[256,32]{0,1:T(8,128)} copy(f32[256,32]{1,0:T(8,128)} %get-tuple-element.9) | data formatting | bytes 65536
  76.0 71.6 %shard_map.61 = f32[8,8,32,128]{3,2,1,0:T(8,128)} custom-call(f32[32,256]{1,0:T(8,128)} %get-tuple-element.4.turned_ref, f32[32,64]{1,0:T(8,128)} %dynamic-slice_bitcast_fusion.two_ref, f32[256,512,128]{2,1,0:T(8,128)} %bitcast.table_ref), custom_call_target="tpu_custom_call" | custom-call | tf_op jit(solution)/shard_map/pallas_call | solution.py:326
  147.6 1.9 %fusion = f32[8,4,128,32,1]{2,3,0,1,4:T(8,128)S(1)} fusion(f32[64,32]{1,0:T(8,128)S(1)} %copy.11, f32[8,8,32,128]{3,2,1,0:T(8,128)} %shard_map.61), kind=kOutput, calls=%fused_computation | convolution fusion | flops 100663296 | bytes 1581056 | tf_op jit(solution)/shard_map/wrbjm,wjc->rbcm/dot_general | solution.py:367
  149.5 0.8 copy.24
Async XLA Ops:
  0.6 0.8 copy-start
  42.3 0.7 copy-start.1

commit v3 on v2

--- a/solution.py
+++ b/solution.py
@@ -56,7 +56,7 @@
     order, rows, cells = flat.shape
     block = min(32, rows)
     return pl.pallas_call(
-        functools.partial(gram_kernel, min(16, block)),
+        functools.partial(gram_kernel, block),
         grid=(rows // block,),
         in_specs=[pl.BlockSpec((order, block, cells), lambda i: (0, i, 0))],
         out_specs=pl.BlockSpec((order, order), lambda i: (0, 0)),
@@ -97,7 +97,7 @@
 
 
 def basis_kernel(
-    narrow, wide, scale, part_ref, prior_ref, basis_ref, turned_ref,
+    narrow, wide, scale, part_ref, prior_ref, turned_ref,
     box_n, mine, box_w, full, square, sn, rn, sw, rw, tw, vw, tn, vn,
 ):
     at, place = lax.axis_index("narrow"), lax.axis_index("wide")
@@ -137,25 +137,24 @@
     for i in range(narrow * wide):
         square[i * small : (i + 1) * small, :] = full[i // wide, i % wide]
     gram = square[...]
-    basis = prior_ref[...]
+    basis = prior_ref[...].T
     rank = basis.shape[1]
     row = lax.broadcasted_iota(jnp.int32, (rank, 1), 0)
     lane = lax.broadcasted_iota(jnp.int32, (rank, rank), 1)
-    square_row = lax.broadcasted_iota(jnp.int32, (rank, rank), 0)
+    unit = jnp.where(lane == lax.broadcasted_iota(jnp.int32, (rank, rank), 0), 1.0, 0.0)
     for _ in range(SUB):
         q = jnp.dot(gram, basis, precision=HIGH, preferred_element_type=F32)
         s = lax.dot_general(q, q, TN, precision=HIGH, preferred_element_type=F32)
-        inverse = jnp.where(lane == square_row, 1.0, 0.0)
+        pair = jnp.concatenate([s, unit], axis=1)
         root = jnp.ones((rank, 1), F32)
         for k in range(rank):
-            pivot = s[k : k + 1, k : k + 1]
-            root = jnp.where(row == k, lax.rsqrt(pivot), root)
-            factor = jnp.where(row > k, s[:, k : k + 1] / pivot, 0.0)
-            inverse = inverse - factor * inverse[k : k + 1, :]
-            s = s - factor * s[k : k + 1, :]
-        inverse = inverse * root
+            line = pair[k : k + 1, :]
+            pivot = line[:, k : k + 1]
+            root = jnp.where(row == k, pivot, root)
+            factor = jnp.where(row > k, pair[:, k : k + 1], 0.0)
+            pair = pair - factor * (line / pivot)
+        inverse = pair[:, rank:] * lax.rsqrt(root)
         basis = lax.dot_general(q, inverse, NT, precision=HIGH, preferred_element_type=F32)
-    basis_ref[...] = basis
     turned_ref[...] = basis.T
 
 
@@ -167,11 +166,8 @@
     return pl.pallas_call(
         functools.partial(basis_kernel, narrow, wide, scale),
         in_specs=[pl.BlockSpec(memory_space=pltpu.VMEM)] * 2,
-        out_specs=[pl.BlockSpec(memory_space=pltpu.VMEM)] * 2,
-        out_shape=(
-            jax.ShapeDtypeStruct((order, rank), F32),
-            jax.ShapeDtypeStruct((rank, order), F32),
-        ),
+        out_specs=pl.BlockSpec(memory_space=pltpu.VMEM),
+        out_shape=jax.ShapeDtypeStruct((rank, order), F32),
         scratch_shapes=[
             pltpu.VMEM((narrow, wide, small, order), F32),
             pltpu.VMEM((wide, small, order), F32),
@@ -184,7 +180,7 @@
             dma((narrow,)), dma((narrow,)),
         ],
         compiler_params=pltpu.CompilerParams(collective_id=1, has_side_effects=True),
-    )(gram.reshape(narrow, wide, small, order), prior)
+    )(gram.reshape(narrow, wide, small, order), prior.T)
 
 
 def project_kernel(
@@ -227,8 +223,7 @@
         slab = width * depth
         chips = narrow // 2
         chip, core = at // 2, lax.rem(at, 2)
-        chunk = 2 if per % 2 == 0 else 1
-        chunks = per // chunk
+        chunk, chunks = 1, per
         flat = second.reshape(rank * slab, cells)
 
         def compute(block, q):
@@ -321,7 +316,7 @@
     per, slab, chips = rank // narrow, width * depth, narrow // 2
     spread = (slab // wide) % 8 == 0
     shape = (wide, per, slab // wide, cells) if spread else (1, per, slab, cells)
-    chunks = per // 2 if per % 2 == 0 else per
+    chunks = per
     dma = pltpu.SemaphoreType.DMA
     out = pl.pallas_call(
         functools.partial(
@@ -359,13 +354,13 @@
 def per_device(narrow, wide, table, prior_one, factor_two, factor_three):
     order, rows_two, rows_three, cells = table.shape
     flat = table.reshape(order, rows_two * rows_three, cells)
-    basis, turned = basis_of(narrow, wide, gram_of(flat), prior_one)
+    turned = basis_of(narrow, wide, gram_of(flat), prior_one)
     at = lax.axis_index("narrow")
     two = lax.dynamic_slice_in_dim(factor_two, at * rows_two, rows_two, 0).T
     spread = project(narrow, wide, turned, two, flat, rows_three)
     three = factor_three.reshape(wide, rows_three, factor_three.shape[1])
     core_out = jnp.einsum("wrbjm,wjc->rbcm", spread, three, precision=HIGH)
-    return core_out, basis
+    return core_out, turned.T
 
 
 def solution(mesh):

time: 152 us -> 152 us (level)
  local copies, waits for them, and re-layouts: 6.85 us -> 4.38 us
  Pallas kernels: 141 us -> 143 us
    pallas_call x1, Pallas kernels: 71.6 us -> 75.7 us  [project(): pl.pallas_call(functools.partial(project_kernel, min(16, block), depth, n...]
    unnamed x7 -> x8, local copies, waits for them, and re-layouts: 5.35 us -> 2.86 us
    pallas_call x1, Pallas kernels: 37.9 us -> 36.2 us  [gram_of(): pl.pallas_call(functools.partial(gram_kernel, block), grid=(rows // block...]
where the time goes in v3:
time: 152 us; the launch traced here: 150 us
  Pallas kernels  143 us (94%)
  local copies, waits for them, and re-layouts  4.38 us (3%)
  matrix products  1.91 us (1%)
    pallas_call x1, Pallas kernels, project(): pl.pallas_call(functools.partial(project_kernel, min(16, block), depth, n...  75.7 us
    pallas_call x1, Pallas kernels, gram_of(): pl.pallas_call(functools.partial(gram_kernel, block), grid=(rows // block...  36.2 us
    pallas_call x1, Pallas kernels, basis_of(): pl.pallas_call(functools.partial(basis_kernel, narrow, wide, scale), in_s...  31.4 us

profile of v3, /device:TPU:0, one launch (start us, length us, event | category | flops | bytes accessed | tf_op | source)
XLA Modules:
  0.0 150.3 jit_solution(5598413393370511400)
XLA Ops:
  0.6 0.0 copy-start
  0.6 0.7 copy-done
  1.4 0.7 dynamic-slice_bitcast_fusion.two_ref
  2.1 0.8 copy.8
  2.9 36.2 %shard_map.59 = f32[256,256]{1,0:T(8,128)S(1)} custom-call(f32[256,512,128]{2,1,0:T(8,128)} %bitcast.table_ref), custom_call_target="tpu_custom_call" | custom-call | tf_op jit(solution)/shard_map/pallas_call | solution.py:58
  39.1 0.0 copy-start.1
  39.1 0.7 copy-done.1
  39.8 31.4 %shard_map.60.turned_ref = f32[32,256]{1,0:T(8,128)} custom-call(f32[4,8,8,256]{3,2,1,0:T(8,128)} %bitcast.22, f32[32,256]{1,0:T(8,128)} %bitcast.25), custom_call_target="tpu_custom_call" | custom-call | tf_op jit(solution)/shard_map/pallas_call | solution.py:166
  71.3 0.0 copy-start.2
  71.3 75.7 %shard_map.61 = f32[8,8,32,128]{3,2,1,0:T(8,128)} custom-call(f32[32,256]{1,0:T(8,128)} %shard_map.60.turned_ref, f32[32,64]{1,0:T(8,128)} %dynamic-slice_bitcast_fusion.two_ref, f32[256,512,128]{2,1,0:T(8,128)} %bitcast.table_ref), custom_call_target="tpu_custom_call" | custom-call | tf_op jit(solution)/shard_map/pallas_call | solution.py:321
  147.0 1.9 %fusion = f32[8,4,128,32,1]{2,3,0,1,4:T(8,128)S(1)} fusion(f32[64,32]{1,0:T(8,128)S(1)} %copy.8, f32[8,8,32,128]{3,2,1,0:T(8,128)} %shard_map.61), kind=kOutput, calls=%fused_computation | convolution fusion | flops 100663296 | bytes 1581056 | tf_op jit(solution)/shard_map/wrbjm,wjc->rbcm/dot_general | solution.py:362
  148.9 0.8 copy.20
  149.7 0.0 copy-done.2
  149.7 0.6 copy.22
Async XLA Ops:
  0.6 0.8 copy-start
  39.1 0.7 copy-start.1
  71.3 78.5 %copy-start.2 = (f32[32,256]{1,0:T(8,128)S(1)}, f32[32,256]{1,0:T(8,128)}, u32[]{:S(2)}) copy-start(f32[32,256]{1,0:T(8,128)} %shard_map.60.turned_ref) | copy-start | bytes 98308
